TPU v7x, 32 devices: a whole 2x2x4 slice. The times are simulated.
32 devices in a mesh: rows: 4 (over y, core), dp: 8 (over z, x).
Axes of the slice: x: 2, y: 2, z: 4, core: 2. Of those that a mesh axis runs over, the one named last changes fastest.
Arguments:
- emb_weight: float32 [8, 6144, 128], P('dp', 'rows'), may hold values from -160 to 160
- emb_grad: bfloat16 [8, 6144, 128], P('dp', 'rows'), may hold values from -6 to 6
- emb_moment: float32 [8, 6144, 128], P('dp', 'rows'), may hold values from -160 to 160
- emb_second: float32 [8, 6144, 128], P('dp', 'rows'), may hold values from 0.1 to 4
- hot_rows: int32 [8, 4, 256], P('dp', 'rows'), may hold values from 0 to 1535
- block_counts: int32 [8, 4], P('dp', 'rows'), may hold values from 1 to 2, as said below
- dense_weight: float32 [512, 256], replicated, may hold values from -8 to 8
- dense_grad: float32 [32, 512, 256], P(('rows', 'dp')), may hold values from -6 to 6
- dense_moment: float32 [512, 256], replicated, may hold values from -900 to 900
- dense_second: float32 [512, 256], replicated, may hold values from 3.2 to 128
Outputs:
- new_weight: float32 [8, 6144, 128], P('dp', 'rows')
- new_moment: float32 [8, 6144, 128], P('dp', 'rows')
- new_second: float32 [8, 6144, 128], P('dp', 'rows')
- hot_cache: bfloat16 [8, 4, 256, 128], P(None, 'rows')
- fresh_dense: float32 [512, 256], replicated
- fresh_moment: float32 [512, 256], replicated
- fresh_second: float32 [512, 256], replicated
Inputs may be any that keep to these rules, and one draw needn't show every extreme that they name: `block_counts`: some table shard has 2 live blocks in every draw. `hot_rows`: entries in dead blocks are ignored.
All inputs are finite; a program needn't handle non-finite values.
Results may differ from a plain program's by a relative error of at most 0.001.
Values may be sent and summed in bfloat16 or wider, within the bound.
A program may use at most 64 MiB of HBM per device.

v0:
```python
import jax
import jax.numpy as jnp
from jax import lax
from jax.sharding import PartitionSpec as P

BLOCK = 128


beta_one = 0.9
beta_two = 0.999
first_fix = 1.0 / (1.0 - 0.9**10)
second_fix = 1.0 / (1.0 - 0.999**10)
epsilon = 1e-06
norm_floor = 1e-06
decay_rate = 0.1
learn_rate = 0.05


def moments(gradient, moment, second):
    new_moment = beta_one * moment + (1.0 - beta_one) * gradient
    new_second = beta_two * second + (1.0 - beta_two) * gradient * gradient
    direction = first_fix * new_moment / (jnp.sqrt(second_fix * new_second) + epsilon)
    return (new_moment, new_second, direction)


def trust_step(weight_sq, update_sq):
    return learn_rate * jnp.sqrt(weight_sq + norm_floor) / jnp.sqrt(update_sq + norm_floor)


def pick_rows(source, row_ids, live_mask):
    picked = jnp.take_along_axis(source, row_ids[:, :, None], axis=1)
    return jnp.where(live_mask, picked, jnp.zeros_like(picked))


def shards(
    emb_weight,
    emb_grad,
    emb_moment,
    emb_second,
    hot_rows,
    block_counts,
    dense_weight,
    dense_grad,
    dense_moment,
    dense_second,
):
    new_moment, new_second, direction = moments(
        emb_grad.astype(jnp.float32), emb_moment, emb_second
    )
    update = direction + decay_rate * emb_weight
    weight_sq = jnp.sum(emb_weight * emb_weight, axis=(1, 2))
    update_sq = jnp.sum(update * update, axis=(1, 2))
    row_ids = hot_rows[:, 0, :]
    live_mask = (
        jnp.arange(row_ids.shape[1], dtype=jnp.int32)[None, :] < BLOCK * block_counts[:, 0][:, None]
    )[:, :, None]
    weight_sq, update_sq = lax.psum((weight_sq, update_sq), "rows")
    summed_grad = lax.psum(dense_grad[0], ("rows", "dp"))
    step_size = trust_step(weight_sq, update_sq)
    new_weight = emb_weight - step_size[:, None, None] * update
    fresh_rows = pick_rows(new_weight, row_ids, live_mask).astype(jnp.bfloat16)
    hot_cache = lax.all_gather(fresh_rows[:, None], "dp", axis=0, tiled=True)
    fresh_moment, fresh_second, heading = moments(summed_grad, dense_moment, dense_second)
    dense_scale = trust_step(jnp.sum(dense_weight * dense_weight), jnp.sum(heading * heading))
    fresh_dense = dense_weight - dense_scale * heading
    return (new_weight, new_moment, new_second, hot_cache, fresh_dense, fresh_moment, fresh_second)


def solution(mesh):
    in_specs = (
        P("dp", "rows", None),
        P("dp", "rows", None),
        P("dp", "rows", None),
        P("dp", "rows", None),
        P("dp", "rows", None),
        P("dp", "rows"),
        P(),
        P(("rows", "dp"), None, None),
        P(),
        P(),
    )
    out_specs = (
        P("dp", "rows", None),
        P("dp", "rows", None),
        P("dp", "rows", None),
        P(None, "rows", None, None),
        P(),
        P(),
        P(),
    )
    return jax.shard_map(shards, mesh=mesh, in_specs=in_specs, out_specs=out_specs, check_vma=False)
```

profile of v0, /device:TPU:0, one launch (start us, length us, event | category | flops | bytes accessed | tf_op | source)
XLA Modules:
  0.0 157.2 jit_solution(17195900723018866183)
XLA Ops:
  7.2 0.0 copy-start.7
  7.2 0.0 all-reduce.3.cloned.1.call-start
  7.2 0.7 all-reduce.3.cloned.1.call-update
  7.9 0.3 copy-done.7
  8.2 0.0 copy-start
  8.2 3.0 %multiply_reduce_fusion = (f32[]{:T(128)}, f32[]{:T(128)}, f32[1,1536,128]{2,1,0:T(8,128)S(1)}, f32[1,1536,128]{2,1,0:T(8,128)S(1)}) fusion(f32[1,1536,128]{2,1,0:T(8,128)} %param.10, bf16[1,1536,128]{2,1,0:T(8,128)(2,1)S(1)} %copy-done.7, f32[1,1536,128]{2,1,0:T(8,128)} %param.12, f32[1,1536,128]{2,1,0:T(8,128)} %param.13), kind=kLoop, calls=%fused_computation.7 | loop fusion | flops 3538942 | bytes 4325384 | tf_op jit(solution)/shard_map/reduce_sum | solution.py:52
  11.1 0.0 copy-start.1
  11.1 0.0 copy-start.2
  11.1 9.0 %all-reduce = (f32[1]{0:T(128)}, f32[1]{0:T(128)}) all-reduce(f32[1]{0:T(128)} %bitcast, f32[1]{0:T(128)} %bitcast.1), channel_id=1, replica_groups=mesh['rows'=4,'dp'=8] {'rows'}, use_global_device_ids=true, to_apply=%region_1.0 | all-reduce | flops 2 | bytes 16 | tf_op jit(solution)/shard_map/psum | solution.py:57
  21.5 0.0 copy-start.8
  21.5 0.6 copy-done.8
  22.8 0.0 copy-done
  22.8 0.4 multiply_subtract_fusion
  23.3 0.0 copy-done.1
  23.3 0.0 copy-done.2
  23.3 0.0 copy-start.3
  23.3 0.0 copy-start.4
  23.3 0.7 gather_fusion
  24.1 0.1 fusion.4
  24.2 32.1 %all_gather.3 = bf16[8,1,256,128]{3,2,1,0:T(8,128)(2,1)S(1)} all-gather(bf16[1,1,256,128]{3,2,1,0:T(8,128)(2,1)S(1)} %fusion.4), channel_id=1, replica_groups=mesh['rows'=4,'dp'=8] {'dp'}, dimensions={0}, use_global_device_ids=true | all-gather | bytes 589824 | tf_op jit(solution)/shard_map/all_gather | solution.py:62
  56.3 0.0 copy-done.4
  56.3 0.7 multiply_reduce_fusion.3
  57.0 0.0 copy-done.3
  57.7 87.8 %all-reduce.3.cloned.1.call-done = f32[512,256]{1,0:T(8,128)} async-done(((f32[512,256]{1,0:T(8,128)}), f32[512,256]{1,0:T(8,128)}) %all-reduce.3.cloned.1.call-update) | async-done | bytes 524304 | tf_op jit(solution)/shard_map/psum | solution.py:58
  145.5 2.3 %multiply_reduce_fusion.2 = (f32[]{:T(128)}, f32[512,256]{1,0:T(8,128)S(1)}, f32[512,256]{1,0:T(8,128)S(1)}) fusion(f32[512,256]{1,0:T(8,128)} %all-reduce.3.cloned.1.call-done, f32[512,256]{1,0:T(8,128)} %param.18, f32[512,256]{1,0:T(8,128)} %param.19), kind=kLoop, calls=%fused_computation.12 | loop fusion | flops 1703935 | bytes 2621444 | tf_op jit(solution)/shard_map/reduce_sum | solution.py:64
  147.8 0.0 copy-start.5
  147.8 0.0 copy-start.6
  148.5 1.0 multiply_subtract_fusion.1
  149.6 0.0 copy-done.5
  149.6 0.0 copy-done.6
  149.6 0.8 copy.21
  (3 shorter events, 0.0 us)
Async XLA Ops:
  7.2 1.0 copy-start.7
  7.2 138.3 %all-reduce.3.cloned.1.call-start = ((), (), s32[]{:S(2)}) async-start(), calls=%async_computation | async-start | bytes 1048576 | tf_op jit(solution)/shard_map/psum | solution.py:58
  8.2 14.7 %copy-start = (f32[1,1536,128]{2,1,0:T(8,128)S(1)}, f32[1,1536,128]{2,1,0:T(8,128)}, u32[]{:S(2)}) copy-start(f32[1,1536,128]{2,1,0:T(8,128)} %param.10) | copy-start | bytes 2359300
  11.1 12.2 %copy-start.1 = (f32[1,1536,128]{2,1,0:T(8,128)}, f32[1,1536,128]{2,1,0:T(8,128)S(1)}, u32[]{:S(2)}) copy-start(f32[1,1536,128]{2,1,0:T(8,128)S(1)} %get-tuple-element.26) | copy-start | bytes 2359300
  11.1 12.2 %copy-start.2 = (f32[1,1536,128]{2,1,0:T(8,128)}, f32[1,1536,128]{2,1,0:T(8,128)S(1)}, u32[]{:S(2)}) copy-start(f32[1,1536,128]{2,1,0:T(8,128)S(1)} %get-tuple-element.27) | copy-start | bytes 2359300
  21.5 0.7 copy-start.8
  23.3 33.7 %copy-start.3 = (f32[1,1536,128]{2,1,0:T(8,128)}, f32[1,1536,128]{2,1,0:T(8,128)S(1)}, u32[]{:S(2)}) copy-start(f32[1,1536,128]{2,1,0:T(8,128)S(1)} %multiply_subtract_fusion) | copy-start | bytes 2359300
  23.3 33.0 %copy-start.4 = (f32[512,256]{1,0:T(8,128)S(1)}, f32[512,256]{1,0:T(8,128)}, u32[]{:S(2)}) copy-start(f32[512,256]{1,0:T(8,128)} %param.16) | copy-start | bytes 1572868
  147.8 1.7 %copy-start.5 = (f32[512,256]{1,0:T(8,128)}, f32[512,256]{1,0:T(8,128)S(1)}, u32[]{:S(2)}) copy-start(f32[512,256]{1,0:T(8,128)S(1)} %get-tuple-element.30) | copy-start | bytes 1572868
  147.8 1.7 %copy-start.6 = (f32[512,256]{1,0:T(8,128)}, f32[512,256]{1,0:T(8,128)S(1)}, u32[]{:S(2)}) copy-start(f32[512,256]{1,0:T(8,128)S(1)} %get-tuple-element.31) | copy-start | bytes 1572868
Sparse Core Ops, SparseCore 0:
  13.3 132.2 all-reduce.2
where the time goes:
time: 157 us
  waiting for transfers between devices  88.5 us (56%)
  blocking collectives  41.1 us (26%)
  between operations  17.5 us (11%)
  other arithmetic  7.64 us (5%)
  local copies, waits for them, and re-layouts  2.45 us (2%)
    psum x1, waiting for transfers between devices, shards(): summed_grad = lax.psum(dense_grad[0], ('rows', 'dp'))  87.8 us
    all_gather x1, blocking collectives, shards(): hot_cache = lax.all_gather(fresh_rows[:, None], 'dp', axis=0, tiled=True)  32.1 us
    psum x1, blocking collectives, shards(): weight_sq, update_sq = lax.psum((weight_sq, update_sq), 'rows')  9.01 us
  transfers between devices with their start and end apart: 1, of which 1 were waited for; matrix products, arithmetic and copies ran while one was open for 3% of the time, Pallas kernels for 0%

commit v1 on v0

v1 whole, which is shorter than its diff:
```python
import functools

import jax
import jax.numpy as jnp
from jax import lax
from jax.experimental import pallas as pl
from jax.experimental.pallas import tpu as pltpu
from jax.sharding import PartitionSpec as P

BLOCK = 128


beta_one = 0.9
beta_two = 0.999
first_fix = 1.0 / (1.0 - 0.9**10)
second_fix = 1.0 / (1.0 - 0.999**10)
epsilon = 1e-06
norm_floor = 1e-06
decay_rate = 0.1
learn_rate = 0.05

MESH = pl.DeviceIdType.MESH
CORES = 2
PAIR = 2
WIRE = jnp.bfloat16


def moments(gradient, moment, second):
    new_moment = beta_one * moment + (1.0 - beta_one) * gradient
    new_second = beta_two * second + (1.0 - beta_two) * gradient * gradient
    direction = first_fix * new_moment / (jnp.sqrt(second_fix * new_second) + epsilon)
    return (new_moment, new_second, direction)


def trust_step(weight_sq, update_sq):
    return learn_rate * jnp.sqrt(weight_sq + norm_floor) / jnp.sqrt(update_sq + norm_floor)


def fold(x):
    return jnp.sum(x.reshape(-1, 8, x.shape[-1]), axis=0)


def full_sum(x):
    return jnp.sum(jnp.sum(x, axis=0, keepdims=True), axis=1, keepdims=True)


def exchange(
    n_rows, n_dp, chunks,
    rows_ref, count_ref, w_hbm, g_hbm, m_hbm, v_hbm, dg_hbm,
    s_ref, G_ref, hot_ref,
    w_buf, g_buf, m_buf, v_buf, u_buf, dg_buf,
    core_out, core_in, plane_out, plane_in, z_buf, sums, hot_w, hot_u,
    load_sem, dload_sem, core_sem, plane_send, plane_recv, up_sem, down_sem, z_recv,
    gather_send, gather_recv, twin_send, twin_recv,
    sum_send, sum_recv, hot_up, hot_down, hot_zrecv, hot_x, hot_xrecv,
):
    r, d = lax.axis_index("rows"), lax.axis_index("dp")
    core, y = lax.rem(r, CORES), lax.div(r, CORES)
    x, z = lax.rem(d, PAIR), lax.div(d, PAIR)
    ys, zs = n_rows // CORES, n_dp // PAIR
    quads = ys * PAIR
    q = y * PAIR + x
    twin = (y * CORES + 1 - core, d)
    side = (r, z * PAIR + 1 - x)
    above, below = (r, d + PAIR), (r, d - PAIR)
    has_above, has_below = z < zs - 1, z > 0

    def plane_peer(k):
        other = lax.rem(q + k, quads)
        oy, ox = lax.div(other, PAIR), lax.rem(other, PAIR)
        return other, (oy * CORES + core, z * PAIR + ox)

    def row_peer(k):
        other = lax.rem(r + k, n_rows)
        return other, (other, d)

    dload = pltpu.make_async_copy(dg_hbm.at[0], dg_buf, dload_sem)
    dload.start()
    span = w_buf.shape[0] // chunks

    def loads(c):
        here = pl.ds(pl.multiple_of(c * span, span), span)
        return [
            pltpu.make_async_copy(src.at[0, here], dst.at[here], load_sem.at[i, c])
            for i, (src, dst) in enumerate(
                ((w_hbm, w_buf), (g_hbm, g_buf), (m_hbm, m_buf), (v_hbm, v_buf))
            )
        ]

    for c in range(chunks):
        for copy in loads(c):
            copy.start()

    barrier = pltpu.get_barrier_semaphore()
    greeted = 0
    for k in range(1, n_rows):
        pl.semaphore_signal(barrier, inc=1, device_id=row_peer(k)[1], device_id_type=MESH)
        greeted += 1
    for oy in range(ys):
        pl.semaphore_signal(
            barrier, inc=1, device_id=(oy * CORES + core, z * PAIR + 1 - x), device_id_type=MESH
        )
        greeted += 1

    @pl.when(has_above)
    def _():
        pl.semaphore_signal(barrier, inc=1, device_id=above, device_id_type=MESH)

    @pl.when(has_below)
    def _():
        pl.semaphore_signal(barrier, inc=1, device_id=below, device_id_type=MESH)

    pl.semaphore_wait(
        barrier, greeted + has_above.astype(jnp.int32) + has_below.astype(jnp.int32)
    )

    half = dg_buf.shape[0] // CORES
    piece = half // quads
    dload.wait()
    theirs = pl.ds(pl.multiple_of((1 - core) * half, half), half)
    mine = pl.ds(pl.multiple_of(core * half, half), half)
    core_out[...] = dg_buf[theirs, :].astype(WIRE)
    core_copy = pltpu.make_async_remote_copy(
        src_ref=core_out, dst_ref=core_in, send_sem=core_sem.at[0], recv_sem=core_sem.at[1],
        device_id=twin, device_id_type=MESH,
    )
    core_copy.start()

    def step(c, carry):
        for copy in loads(c):
            copy.wait()
        wsq, usq = carry
        here = pl.ds(pl.multiple_of(c * span, span), span)
        w = w_buf[here, :]
        _, _, direction = moments(g_buf[here, :].astype(jnp.float32), m_buf[here, :], v_buf[here, :])
        u = direction + decay_rate * w
        u_buf[here, :] = u
        return wsq + fold(w * w), usq + fold(u * u)

    zero = jnp.zeros((8, w_buf.shape[1]), jnp.float32)
    wsq, usq = lax.fori_loop(0, chunks, step, (zero, zero))
    sums[r, 0] = wsq
    sums[r, 1] = usq

    def sum_copy(k, slot):
        return pltpu.make_async_remote_copy(
            src_ref=sums.at[slot], dst_ref=sums.at[slot],
            send_sem=sum_send.at[k], recv_sem=sum_recv.at[slot],
            device_id=row_peer(k)[1], device_id_type=MESH,
        )

    for k in range(1, n_rows):
        sum_copy(k, r).start()

    core_copy.wait()
    pair_sum = dg_buf[mine, :] + core_in[...].astype(jnp.float32)
    dg_buf[mine, :] = pair_sum
    plane_out[...] = pair_sum.astype(WIRE).reshape(plane_out.shape)

    def plane_copy(k, src_slot, dst_slot):
        return pltpu.make_async_remote_copy(
            src_ref=plane_out.at[src_slot], dst_ref=plane_in.at[dst_slot],
            send_sem=plane_send.at[k], recv_sem=plane_recv.at[dst_slot],
            device_id=plane_peer(k)[1], device_id_type=MESH,
        )

    for k in range(1, quads):
        plane_copy(k, plane_peer(k)[0], q).start()

    hot_n = hot_w.shape[0]

    def pick(j, carry):
        for i in range(8):
            at = rows_ref[0, 0, j * 8 + i]
            hot_w[pl.ds(j * 8 + i, 1), :] = w_buf[pl.ds(at, 1), :]
            hot_u[pl.ds(j * 8 + i, 1), :] = u_buf[pl.ds(at, 1), :]
        return carry

    lax.fori_loop(0, hot_n // 8, pick, 0)
    for k in range(1, n_rows):
        sum_copy(k, row_peer(k)[0]).wait_recv()
    total = jnp.sum(sums[...], axis=0)
    scale = trust_step(full_sum(total[0]), full_sum(total[1]))
    s_ref[...] = jnp.broadcast_to(scale, s_ref.shape)
    fresh = hot_w[...] - scale * hot_u[...]
    live = lax.broadcasted_iota(jnp.int32, fresh.shape, 0) < BLOCK * count_ref[0, 0]
    hot_ref[d, 0] = jnp.where(live, fresh, 0.0).astype(hot_ref.dtype)

    def hot_copy(block, send, recv, target):
        return pltpu.make_async_remote_copy(
            src_ref=hot_ref.at[block, 0], dst_ref=hot_ref.at[block, 0],
            send_sem=send, recv_sem=recv, device_id=target, device_id_type=MESH,
        )

    def hot_above(b):
        return hot_copy(b * PAIR + x, hot_up.at[b], hot_zrecv.at[b], above)

    def hot_below(b):
        return hot_copy(b * PAIR + x, hot_down.at[b], hot_zrecv.at[b], below)

    def hot_side(b):
        return hot_copy(b * PAIR + x, hot_x.at[b], hot_xrecv.at[b], side)

    def hot_from_side(b):
        return hot_copy(b * PAIR + 1 - x, hot_x.at[b], hot_xrecv.at[b], side)

    def z_copy(b, send, target):
        return pltpu.make_async_remote_copy(
            src_ref=z_buf.at[b], dst_ref=z_buf.at[b],
            send_sem=send.at[b], recv_sem=z_recv.at[b], device_id=target, device_id_type=MESH,
        )

    def relay(b, upward, downward, sidewards):
        if upward is not None:
            @pl.when(has_above)
            def _():
                upward(b).start()
        if downward is not None:
            @pl.when(has_below)
            def _():
                downward(b).start()
        if sidewards is not None:
            sidewards(b).start()

    z_above = lambda b: z_copy(b, up_sem, above)
    z_below = lambda b: z_copy(b, down_sem, below)
    relay(z, hot_above, hot_below, hot_side)

    for k in range(1, quads):
        plane_copy(k, 0, plane_peer(k)[0]).wait_recv()
    own = dg_buf[pl.ds(pl.multiple_of(core * half + q * piece, piece), piece), :]
    for k in range(1, quads):
        own = own + plane_in[plane_peer(k)[0]].astype(jnp.float32)
    z_buf[z] = own.astype(WIRE)
    relay(z, z_above, z_below, None)

    def both_ways(k, upward, downward, sidewards):
        low, high = z - k, z + k

        @pl.when(low >= 0)
        def _():
            upward(low).wait_recv()
            relay(low, upward, None, sidewards)

        @pl.when(high < zs)
        def _():
            downward(high).wait_recv()
            relay(high, None, downward, sidewards)

    for k in range(1, zs):
        both_ways(k, z_above, z_below, None)
        both_ways(k, hot_above, hot_below, hot_side)

    reduced = z_buf[0].astype(jnp.float32)
    for b in range(1, zs):
        reduced = reduced + z_buf[b].astype(jnp.float32)

    def slot(core_at, quad_at):
        return pl.ds(pl.multiple_of(core_at * half + quad_at * piece, piece), piece)

    G_ref[slot(core, q), :] = reduced.astype(WIRE)

    def gather_copy(k, quad_at):
        return pltpu.make_async_remote_copy(
            src_ref=G_ref.at[slot(core, quad_at)], dst_ref=G_ref.at[slot(core, quad_at)],
            send_sem=gather_send.at[k], recv_sem=gather_recv.at[quad_at],
            device_id=plane_peer(k)[1], device_id_type=MESH,
        )

    def twin_copy(core_at, quad_at):
        return pltpu.make_async_remote_copy(
            src_ref=G_ref.at[slot(core_at, quad_at)], dst_ref=G_ref.at[slot(core_at, quad_at)],
            send_sem=twin_send.at[quad_at], recv_sem=twin_recv.at[quad_at],
            device_id=twin, device_id_type=MESH,
        )

    for k in range(1, quads):
        gather_copy(k, q).start()
    twin_copy(core, q).start()
    for k in range(1, quads):
        other = plane_peer(k)[0]
        gather_copy(k, other).wait_recv()
        twin_copy(core, other).start()

    for b in range(zs):
        hot_from_side(b).wait_recv()
    for b in range(quads):
        twin_copy(1 - core, b).wait_recv()
    for b in range(quads):
        twin_copy(core, b).wait_send()
    for k in range(1, quads):
        gather_copy(k, q).wait_send()
        plane_copy(k, plane_peer(k)[0], q).wait_send()
    for k in range(1, n_rows):
        sum_copy(k, r).wait_send()
    for b in range(zs):
        hot_side(b).wait_send()

        @pl.when(jnp.logical_and(has_above, b <= z))
        def _():
            hot_above(b).wait_send()
            z_above(b).wait_send()

        @pl.when(jnp.logical_and(has_below, b >= z))
        def _():
            hot_below(b).wait_send()
            z_below(b).wait_send()


def shards(
    n_rows,
    n_dp,
    emb_weight,
    emb_grad,
    emb_moment,
    emb_second,
    hot_rows,
    block_counts,
    dense_weight,
    dense_grad,
    dense_moment,
    dense_second,
):
    _, rs, e = emb_weight.shape
    din, dout = dense_weight.shape
    hot_n = hot_rows.shape[2]
    quads, zs = n_rows // CORES * PAIR, n_dp // PAIR
    half = din // CORES
    piece = half // quads
    chunks = 6 if rs % (6 * 16) == 0 else 1
    f32 = jnp.float32
    dma = pltpu.SemaphoreType.DMA
    vmem = pl.BlockSpec(memory_space=pltpu.VMEM)
    smem = pl.BlockSpec(memory_space=pltpu.SMEM)
    hbm = pl.BlockSpec(memory_space=pl.ANY)
    step_size, summed_grad, hot_cache = pl.pallas_call(
        functools.partial(exchange, n_rows, n_dp, chunks),
        out_shape=(
            jax.ShapeDtypeStruct((8, e), f32),
            jax.ShapeDtypeStruct((din, dout), WIRE),
            jax.ShapeDtypeStruct((n_dp, 1, hot_n, e), jnp.bfloat16),
        ),
        in_specs=[smem, smem] + [hbm] * 5,
        out_specs=(vmem, vmem, vmem),
        scratch_shapes=[
            pltpu.VMEM((rs, e), f32),
            pltpu.VMEM((rs, e), emb_grad.dtype),
            pltpu.VMEM((rs, e), f32),
            pltpu.VMEM((rs, e), f32),
            pltpu.VMEM((rs, e), f32),
            pltpu.VMEM((din, dout), f32),
            pltpu.VMEM((half, dout), WIRE),
            pltpu.VMEM((half, dout), WIRE),
            pltpu.VMEM((quads, piece, dout), WIRE),
            pltpu.VMEM((quads, piece, dout), WIRE),
            pltpu.VMEM((zs, piece, dout), WIRE),
            pltpu.VMEM((n_rows, 2, 8, e), f32),
            pltpu.VMEM((hot_n, e), f32),
            pltpu.VMEM((hot_n, e), f32),
            dma((4, chunks)),
            dma,
            dma((2,)),
            dma((quads,)),
            dma((quads,)),
            dma((zs,)),
            dma((zs,)),
            dma((zs,)),
            dma((quads,)),
            dma((quads,)),
            dma((quads,)),
            dma((quads,)),
            dma((n_rows,)),
            dma((n_rows,)),
            dma((zs,)),
            dma((zs,)),
            dma((zs,)),
            dma((zs,)),
            dma((zs,)),
        ],
        compiler_params=pltpu.CompilerParams(
            collective_id=0, has_side_effects=True, vmem_limit_bytes=24 * 1024 * 1024
        ),
        name="exchange",
    )(hot_rows, block_counts, emb_weight, emb_grad, emb_moment, emb_second, dense_grad)

    new_moment, new_second, direction = moments(
        emb_grad.astype(f32), emb_moment, emb_second
    )
    update = direction + decay_rate * emb_weight
    new_weight = emb_weight - step_size[0, 0] * update
    fresh_moment, fresh_second, heading = moments(
        summed_grad.astype(f32), dense_moment, dense_second
    )
    dense_scale = trust_step(jnp.sum(dense_weight * dense_weight), jnp.sum(heading * heading))
    fresh_dense = dense_weight - dense_scale * heading
    return (new_weight, new_moment, new_second, hot_cache, fresh_dense, fresh_moment, fresh_second)


def solution(mesh):
    in_specs = (
        P("dp", "rows", None),
        P("dp", "rows", None),
        P("dp", "rows", None),
        P("dp", "rows", None),
        P("dp", "rows", None),
        P("dp", "rows"),
        P(),
        P(("rows", "dp"), None, None),
        P(),
        P(),
    )
    out_specs = (
        P("dp", "rows", None),
        P("dp", "rows", None),
        P("dp", "rows", None),
        P(None, "rows", None, None),
        P(),
        P(),
        P(),
    )
    body = functools.partial(shards, mesh.shape["rows"], mesh.shape["dp"])
    return jax.shard_map(body, mesh=mesh, in_specs=in_specs, out_specs=out_specs, check_vma=False)
```

time: 157 us -> 45.6 us (0.29)
  waiting for transfers between devices: 88.5 us -> 0 us
  blocking collectives: 41.1 us -> 0 us
  Pallas kernels: 0 us -> 30.4 us
  between operations: 17.5 us -> 2.73 us
  local copies, waits for them, and re-layouts: 2.45 us -> 6.77 us
  other arithmetic: 7.64 us -> 5.3 us
    psum x1 -> x0, waiting for transfers between devices: 87.8 us -> none  [shards(): summed_grad = lax.psum(dense_grad[0], ('rows', 'dp'))]
    all_gather x1 -> x0, blocking collectives: 32.1 us -> none  [shards(): hot_cache = lax.all_gather(fresh_rows[:, None], 'dp', axis=0, tiled=True)]
    pallas_call x0 -> x1, Pallas kernels: none -> 30.4 us  [shards(): pl.pallas_call(functools.partial(exchange, n_rows, n_dp, chunks), out_sha...]
    psum x1 -> x0, blocking collectives: 9.01 us -> none  [shards(): weight_sq, update_sq = lax.psum((weight_sq, update_sq), 'rows')]
    unnamed x19 -> x23, local copies, waits for them, and re-layouts: 1.71 us -> 6.25 us
    reduce_sum x1 -> x0, other arithmetic: 2.96 us -> none  [shards(): update_sq = jnp.sum(update * update, axis=(1, 2))]
    sub x1, other arithmetic: 0.42 us -> 2.54 us  [shards(): new_weight = emb_weight - step_size[0, 0] * update]
  transfers between devices with their start and end apart: 1 -> 0, of which waited for: 1 -> 0; matrix products, arithmetic and copies ran while one was open for 3% -> 0% of each run, Pallas kernels for 0% -> 0%
where the time goes in v1:
time: 45.6 us; the launch traced here: 45.2 us
  Pallas kernels  30.4 us (67%)
  local copies, waits for them, and re-layouts  6.77 us (15%)
  other arithmetic  5.3 us (12%)
  between operations  2.73 us (6%)
    pallas_call x1, Pallas kernels, shards(): pl.pallas_call(functools.partial(exchange, n_rows, n_dp, chunks), out_sha...  30.4 us
    unnamed x23, local copies, waits for them, and re-layouts  6.25 us
    sub x1, other arithmetic, shards(): new_weight = emb_weight - step_size[0, 0] * update  2.54 us
    sub x1, other arithmetic, shards(): fresh_dense = dense_weight - dense_scale * heading  1.04 us
    reduce_sum x1, other arithmetic, shards(): jnp.sum(heading * heading)  0.98 us

profile of v1, /device:TPU:0, one launch (start us, length us, event | category | flops | bytes accessed | tf_op | source)
XLA Modules:
  0.0 45.2 jit_solution(3942785481770995710)
XLA Ops:
  0.6 0.0 copy-start.5
  1.3 0.0 copy-done.5
  1.3 0.0 copy-start
  1.3 1.1 %copy-done = f32[1,1536,128]{2,1,0:T(8,128)S(1)} copy-done((f32[1,1536,128]{2,1,0:T(8,128)S(1)}, f32[1,1536,128]{2,1,0:T(8,128)}, u32[]{:S(2)}) %copy-start) | copy-done | bytes 786456
  2.4 0.0 copy-start.1
  2.5 1.1 %copy-done.1 = f32[1,1536,128]{2,1,0:T(8,128)S(1)} copy-done((f32[1,1536,128]{2,1,0:T(8,128)S(1)}, f32[1,1536,128]{2,1,0:T(8,128)}, u32[]{:S(2)}) %copy-start.1) | copy-done | bytes 786456
  3.6 0.0 copy-start.2
  3.6 1.1 %copy-done.2 = f32[1,1536,128]{2,1,0:T(8,128)S(1)} copy-done((f32[1,1536,128]{2,1,0:T(8,128)S(1)}, f32[1,1536,128]{2,1,0:T(8,128)}, u32[]{:S(2)}) %copy-start.2) | copy-done | bytes 786456
  4.7 0.0 copy-start.3
  4.7 1.0 %copy-done.3 = bf16[1,1536,128]{2,1,0:T(8,128)(2,1)S(1)} copy-done((bf16[1,1536,128]{2,1,0:T(8,128)(2,1)S(1)}, bf16[1,1536,128]{2,1,0:T(8,128)(2,1)}, u32[]{:S(2)}) %copy-start.3) | copy-done | bytes 393240
  5.7 0.0 copy-start.4
  5.7 1.0 %copy-done.4 = f32[1,512,256]{2,1,0:T(8,128)S(1)} copy-done((f32[1,512,256]{2,1,0:T(8,128)S(1)}, f32[1,512,256]{2,1,0:T(8,128)}, u32[]{:S(2)}) %copy-start.4) | copy-done | bytes 524312
  6.8 30.4 %exchange.1 = (f32[8,128]{1,0:T(8,128)S(1)}, bf16[512,256]{1,0:T(8,128)(2,1)S(1)}, bf16[8,1,256,128]{3,2,1,0:T(8,128)(2,1)S(1)}) custom-call(s32[1,1,256]{2,1,0:T(1,128)S(1)} %copy-done.5, s32[1,1]{1,0:T(1,128)S(6)} %copy.18.count_ref, f32[1,1536,128]{2,1,0:T(8,128)S(1)} %copy-done, bf16[1,1536,128]{2,1,0:T(8,128)(2,1)S(1)} %copy-done.3, ...), custom_call_target="tpu_custom_call" | custom-call | tf_op jit(solution)/shard_map/exchange/pallas_call | solution.py:336
  37.2 0.5 %slice.3 = f32[1,1]{1,0:T(1,128)} slice(f32[8,128]{1,0:T(8,128)S(1)} %get-tuple-element.10), slice={[0:1], [0:1]} | slice | bytes 8 | tf_op jit(solution)/shard_map/slice | solution.py:390
  37.7 0.0 copy-start.8
  37.7 0.0 copy-start.10
  37.7 2.5 %multiply_subtract_fusion = (f32[1,1536,128]{2,1,0:T(8,128)}, f32[1,1536,128]{2,1,0:T(8,128)}, f32[1,1536,128]{2,1,0:T(8,128)}) fusion(f32[1,1536,128]{2,1,0:T(8,128)S(1)} %copy-done, f32[]{:T(128)} %bitcast, bf16[1,1536,128]{2,1,0:T(8,128)(2,1)S(1)} %copy-done.3, f32[1,1536,128]{2,1,0:T(8,128)S(1)} %copy-done.1, f32[1,1536,128]{2,1,0:T(8,128)S(1)} %copy-done.2), kind=kLoop, calls=%fused_computation.5 | loop fusion | flops 3145728 | bytes 5111812 | tf_op jit(solution)/shard_map/sub | solution.py:390
  40.3 0.0 copy-start.9
  40.3 0.0 copy-done.8
  40.3 0.7 %multiply_reduce_fusion.1 = f32[]{:T(128)} fusion(f32[512,256]{1,0:T(8,128)S(1)} %copy-done.8), kind=kLoop, calls=%fused_computation.12 | loop fusion | flops 262143 | bytes 524292 | tf_op jit(solution)/shard_map/reduce_sum | solution.py:394
  41.7 0.0 copy-done.10
  41.7 0.0 copy-done.9
  41.7 1.0 %multiply_reduce_fusion = (f32[]{:T(128)}, f32[512,256]{1,0:T(8,128)S(1)}, f32[512,256]{1,0:T(8,128)S(1)}) fusion(bf16[512,256]{1,0:T(8,128)(2,1)S(1)} %get-tuple-element.12, f32[512,256]{1,0:T(8,128)S(1)} %copy-done.9, f32[512,256]{1,0:T(8,128)S(1)} %copy-done.10), kind=kLoop, calls=%fused_computation.10 | loop fusion | flops 1835007 | bytes 2359300 | tf_op jit(solution)/shard_map/reduce_sum | solution.py:394
  42.7 0.0 copy-start.6
  42.7 0.0 copy-start.7
  43.4 1.0 %multiply_subtract_fusion.1 = f32[512,256]{1,0:T(8,128)} fusion(f32[512,256]{1,0:T(8,128)S(1)} %copy-done.8, f32[]{:T(128)S(6)} %div.11, f32[512,256]{1,0:T(8,128)S(1)} %get-tuple-element.32, f32[512,256]{1,0:T(8,128)S(1)} %get-tuple-element.31), kind=kLoop, calls=%fused_computation.9 | loop fusion | flops 786432 | bytes 2097156 | tf_op jit(solution)/shard_map/sub | solution.py:395
  44.4 0.0 copy-done.6
  44.4 0.0 copy-done.7
  44.4 0.8 %copy.19 = bf16[8,1,256,128]{3,2,1,0:T(8,128)(2,1)} copy(bf16[8,1,256,128]{3,2,1,0:T(8,128)(2,1)S(1)} %get-tuple-element.29) | data formatting | bytes 1048576
Async XLA Ops:
  0.6 0.7 %copy-start.5 = (s32[1,1,256]{2,1,0:T(1,128)S(1)}, s32[1,1,256]{2,1,0:T(1,128)}, u32[]{:S(2)}) copy-start(s32[1,1,256]{2,1,0:T(1,128)} %rows_ref.1) | copy-start | bytes 3076
  1.3 1.1 %copy-start = (f32[1,1536,128]{2,1,0:T(8,128)S(1)}, f32[1,1536,128]{2,1,0:T(8,128)}, u32[]{:S(2)}) copy-start(f32[1,1536,128]{2,1,0:T(8,128)} %w_hbm.1) | copy-start | bytes 2359300
  2.4 1.1 %copy-start.1 = (f32[1,1536,128]{2,1,0:T(8,128)S(1)}, f32[1,1536,128]{2,1,0:T(8,128)}, u32[]{:S(2)}) copy-start(f32[1,1536,128]{2,1,0:T(8,128)} %m_hbm.1) | copy-start | bytes 2359300
  3.6 1.1 %copy-start.2 = (f32[1,1536,128]{2,1,0:T(8,128)S(1)}, f32[1,1536,128]{2,1,0:T(8,128)}, u32[]{:S(2)}) copy-start(f32[1,1536,128]{2,1,0:T(8,128)} %v_hbm.1) | copy-start | bytes 2359300
  4.7 1.0 %copy-start.3 = (bf16[1,1536,128]{2,1,0:T(8,128)(2,1)S(1)}, bf16[1,1536,128]{2,1,0:T(8,128)(2,1)}, u32[]{:S(2)}) copy-start(bf16[1,1536,128]{2,1,0:T(8,128)(2,1)} %g_hbm.1) | copy-start | bytes 1179652
  5.7 1.0 %copy-start.4 = (f32[1,512,256]{2,1,0:T(8,128)S(1)}, f32[1,512,256]{2,1,0:T(8,128)}, u32[]{:S(2)}) copy-start(f32[1,512,256]{2,1,0:T(8,128)} %dg_hbm.1) | copy-start | bytes 1572868
  37.7 2.5 %copy-start.8 = (f32[512,256]{1,0:T(8,128)S(1)}, f32[512,256]{1,0:T(8,128)}, u32[]{:S(2)}) copy-start(f32[512,256]{1,0:T(8,128)} %param.16) | copy-start | bytes 1572868
  37.7 4.0 %copy-start.10 = (f32[512,256]{1,0:T(8,128)S(1)}, f32[512,256]{1,0:T(8,128)}, u32[]{:S(2)}) copy-start(f32[512,256]{1,0:T(8,128)} %param.19) | copy-start | bytes 1572868
  40.3 1.4 %copy-start.9 = (f32[512,256]{1,0:T(8,128)S(1)}, f32[512,256]{1,0:T(8,128)}, u32[]{:S(2)}) copy-start(f32[512,256]{1,0:T(8,128)} %param.18) | copy-start | bytes 1572868
  42.7 1.7 %copy-start.6 = (f32[512,256]{1,0:T(8,128)}, f32[512,256]{1,0:T(8,128)S(1)}, u32[]{:S(2)}) copy-start(f32[512,256]{1,0:T(8,128)S(1)} %get-tuple-element.31) | copy-start | bytes 1572868
  42.7 1.7 %copy-start.7 = (f32[512,256]{1,0:T(8,128)}, f32[512,256]{1,0:T(8,128)S(1)}, u32[]{:S(2)}) copy-start(f32[512,256]{1,0:T(8,128)S(1)} %get-tuple-element.32) | copy-start | bytes 1572868

commit v2 on v1

v2 whole, which is shorter than its diff:
```python
import functools

import jax
import jax.numpy as jnp
from jax import lax
from jax.experimental import pallas as pl
from jax.experimental.pallas import tpu as pltpu
from jax.sharding import PartitionSpec as P

BLOCK = 128


beta_one = 0.9
beta_two = 0.999
first_fix = 1.0 / (1.0 - 0.9**10)
second_fix = 1.0 / (1.0 - 0.999**10)
epsilon = 1e-06
norm_floor = 1e-06
decay_rate = 0.1
learn_rate = 0.05

MESH = pl.DeviceIdType.MESH
CORES = 2
PAIR = 2
WIRE = jnp.bfloat16
EXCHANGE_LIMIT = 40 * 1024 * 1024
WRITE_LIMIT = 1024 * 1024


def moments(gradient, moment, second):
    new_moment = beta_one * moment + (1.0 - beta_one) * gradient
    new_second = beta_two * second + (1.0 - beta_two) * gradient * gradient
    direction = first_fix * new_moment / (jnp.sqrt(second_fix * new_second) + epsilon)
    return (new_moment, new_second, direction)


def trust_step(weight_sq, update_sq):
    return learn_rate * jnp.sqrt(weight_sq + norm_floor) / jnp.sqrt(update_sq + norm_floor)


def fold(x):
    return jnp.sum(x.reshape(-1, 8, x.shape[-1]), axis=0)


def full_sum(x):
    return jnp.sum(jnp.sum(x, axis=0, keepdims=True), axis=1, keepdims=True)


def loop(start, stop, body):
    if stop - start <= 8:
        for i in range(start, stop):
            body(i)
    else:
        lax.fori_loop(start, stop, lambda i, carry: (body(i), carry)[1], 0)


def exchange(
    n_rows, n_dp, chunks, hot_first, hot_chunks, z_chunks,
    count_ref, rows_hbm, w_hbm, g_hbm, m_hbm, v_hbm, dg_hbm, dw_hbm, dm_hbm, dv_hbm,
    w_out, m_out, v_out, hot_ref, dw_out, dm_out, dv_out,
    rows_ref, w_buf, g_buf, m_buf, v_buf, u_buf, dg_buf, dw_buf, dm_buf, dv_buf, G_ref, U_buf,
    core_out, core_in, plane_out, plane_in, z_buf, sums, usqs, hot_w, hot_u,
    load_sem, dload_sem, core_send, core_recv, plane_send, plane_recv, up_sem, down_sem, z_recv,
    gather_send, gather_recv, twin_send, twin_recv,
    sum_send, sum_recv, hot_up, hot_down, hot_x, hot_recv,
):
    r, d = lax.axis_index("rows"), lax.axis_index("dp")
    core, y = lax.rem(r, CORES), lax.div(r, CORES)
    x, z = lax.rem(d, PAIR), lax.div(d, PAIR)
    ys, zs = n_rows // CORES, n_dp // PAIR
    quads = ys * PAIR
    q = y * PAIR + x
    twin = (y * CORES + 1 - core, d)
    side = (r, z * PAIR + 1 - x)
    above, below = (r, d + PAIR), (r, d - PAIR)
    has_above, has_below = z < zs - 1, z > 0

    def plane_peer(k):
        other = lax.rem(q + k, quads)
        oy, ox = lax.div(other, PAIR), lax.rem(other, PAIR)
        return other, (oy * CORES + core, z * PAIR + ox)

    def row_peer(k):
        other = lax.rem(r + k, n_rows)
        return other, (other, d)

    dloads = [
        pltpu.make_async_copy(src, dst, dload_sem.at[i])
        for i, (src, dst) in enumerate(
            (
                (dg_hbm.at[0], dg_buf), (dw_hbm, dw_buf), (dm_hbm, dm_buf), (dv_hbm, dv_buf),
                (rows_hbm, rows_ref),
            )
        )
    ]
    dloads[0].start()
    span = w_buf.shape[0] // chunks

    def loads(c):
        here = pl.ds(pl.multiple_of(c * span, span), span)
        return [
            pltpu.make_async_copy(src.at[0, here], dst.at[here], load_sem.at[i, c])
            for i, (src, dst) in enumerate(
                ((w_hbm, w_buf), (g_hbm, g_buf), (m_hbm, m_buf), (v_hbm, v_buf))
            )
        ]

    for c in range(chunks):
        for copy in loads(c):
            copy.start()
    for copy in dloads[1:]:
        copy.start()

    barrier = pltpu.get_barrier_semaphore()
    greeted = 0
    for k in range(1, n_rows):
        pl.semaphore_signal(barrier, inc=1, device_id=row_peer(k)[1], device_id_type=MESH)
        greeted += 1
    for oy in range(ys):
        pl.semaphore_signal(
            barrier, inc=1, device_id=(oy * CORES + core, z * PAIR + 1 - x), device_id_type=MESH
        )
        greeted += 1

    @pl.when(has_above)
    def _():
        pl.semaphore_signal(barrier, inc=1, device_id=above, device_id_type=MESH)

    @pl.when(has_below)
    def _():
        pl.semaphore_signal(barrier, inc=1, device_id=below, device_id_type=MESH)

    pl.semaphore_wait(
        barrier, greeted + has_above.astype(jnp.int32) + has_below.astype(jnp.int32)
    )

    half = dg_buf.shape[0] // CORES
    piece = half // quads

    def slot(core_at, quad_at):
        return pl.ds(pl.multiple_of(core_at * half + quad_at * piece, piece), piece)

    def core_copy(quad_at):
        return pltpu.make_async_remote_copy(
            src_ref=core_out.at[quad_at], dst_ref=core_in.at[quad_at],
            send_sem=core_send.at[quad_at], recv_sem=core_recv.at[quad_at],
            device_id=twin, device_id_type=MESH,
        )

    dloads[0].wait()
    for k in range(1, quads + 1):
        other = lax.rem(q + k, quads)
        core_out[other] = dg_buf[slot(1 - core, other), :].astype(WIRE)
        core_copy(other).start()

    def step(c, carry):
        for copy in loads(c):
            copy.wait()
        wsq, usq = carry
        here = pl.ds(pl.multiple_of(c * span, span), span)
        w = w_buf[here, :]
        m, v, direction = moments(g_buf[here, :].astype(jnp.float32), m_buf[here, :], v_buf[here, :])
        u = direction + decay_rate * w
        u_buf[here, :] = u
        m_out[0, here, :] = m
        v_out[0, here, :] = v
        return wsq + fold(w * w), usq + fold(u * u)

    def plane_copy(k, src_slot, dst_slot):
        return pltpu.make_async_remote_copy(
            src_ref=plane_out.at[src_slot], dst_ref=plane_in.at[dst_slot],
            send_sem=plane_send.at[k], recv_sem=plane_recv.at[dst_slot],
            device_id=plane_peer(k)[1], device_id_type=MESH,
        )

    zero = jnp.zeros((8, w_buf.shape[1]), jnp.float32)
    early = chunks // 2
    partial = lax.fori_loop(0, early, step, (zero, zero))

    for k in range(1, quads):
        other = plane_peer(k)[0]
        core_copy(other).wait_recv()
        plane_out[other] = (
            dg_buf[slot(core, other), :] + core_in[other].astype(jnp.float32)
        ).astype(WIRE)
        plane_copy(k, other, q).start()

    wsq, usq = lax.fori_loop(early, chunks, step, partial)
    sums[r, 0] = wsq
    sums[r, 1] = usq

    def sum_copy(k, slot):
        return pltpu.make_async_remote_copy(
            src_ref=sums.at[slot], dst_ref=sums.at[slot],
            send_sem=sum_send.at[k], recv_sem=sum_recv.at[slot],
            device_id=row_peer(k)[1], device_id_type=MESH,
        )

    for k in range(1, n_rows):
        sum_copy(k, r).start()

    core_copy(q).wait_recv()
    own = dg_buf[slot(core, q), :] + core_in[q].astype(jnp.float32)
    for k in range(1, quads):
        other = plane_peer(k)[0]
        plane_copy(k, 0, other).wait_recv()
        own = own + plane_in[other].astype(jnp.float32)
    z_buf[z] = own.astype(WIRE).reshape(z_buf.shape[1:])

    def z_copy(b, c, send, target):
        return pltpu.make_async_remote_copy(
            src_ref=z_buf.at[b, c], dst_ref=z_buf.at[b, c],
            send_sem=send.at[b, c], recv_sem=z_recv.at[b, c], device_id=target, device_id_type=MESH,
        )

    hot_rows_at = hot_ref.shape[2] // hot_chunks

    def hot_copy(block, c, send, target):
        here = pl.ds(c * hot_rows_at, hot_rows_at)
        return pltpu.make_async_remote_copy(
            src_ref=hot_ref.at[block, 0, here], dst_ref=hot_ref.at[block, 0, here],
            send_sem=send.at[block, c], recv_sem=hot_recv.at[block, c],
            device_id=target, device_id_type=MESH,
        )

    def on(condition, action):
        @pl.when(condition)
        def _():
            action()

    def z_all(b, up, down):
        for c in range(z_chunks):
            if up:
                z_copy(b, c, up_sem, above).start()
            if down:
                z_copy(b, c, down_sem, below).start()

    on(has_above, lambda: z_all(z, True, False))
    on(has_below, lambda: z_all(z, False, True))

    hot_n = hot_w.shape[0]

    def pick(j, carry):
        for i in range(8):
            at = rows_ref[0, 0, j * 8 + i]
            hot_w[pl.ds(j * 8 + i, 1), :] = w_buf[pl.ds(at, 1), :]
            hot_u[pl.ds(j * 8 + i, 1), :] = u_buf[pl.ds(at, 1), :]
        return carry

    for copy in dloads[4:]:
        copy.wait()
    lax.fori_loop(0, hot_n // 8, pick, 0)
    for k in range(1, n_rows):
        sum_copy(k, row_peer(k)[0]).wait_recv()
    total = jnp.sum(sums[...], axis=0)
    scale = trust_step(full_sum(total[0]), full_sum(total[1]))
    fresh = hot_w[...] - scale * hot_u[...]
    live = lax.broadcasted_iota(jnp.int32, fresh.shape, 0) < BLOCK * count_ref[0, 0]
    hot_ref[d, 0] = jnp.where(live, fresh, 0.0).astype(hot_ref.dtype)

    order = list(range(hot_first, hot_chunks)) + list(range(hot_first))
    for c in order:
        hot_copy(d, c, hot_x, side).start()
        on(has_above, lambda: hot_copy(d, c, hot_up, above).start())
        on(has_below, lambda: hot_copy(d, c, hot_down, below).start())

    def renew(c, carry):
        here = pl.ds(pl.multiple_of(c * span, span), span)
        w_out[0, here, :] = w_buf[here, :] - scale * u_buf[here, :]
        return carry

    lax.fori_loop(0, chunks, renew, 0)

    across = z * PAIR + 1 - x
    for c in range(hot_first, hot_chunks):
        hot_copy(across, c, hot_x, side).wait_recv()
        on(has_above, lambda: hot_copy(across, c, hot_up, above).start())
        on(has_below, lambda: hot_copy(across, c, hot_down, below).start())

    def both_ways(k):
        low, high = z - k, z + k

        def dense_from(b, send, target, onward):
            def run():
                for c in range(z_chunks):
                    z_copy(b, c, send, target).wait_recv()
                    on(onward, lambda: z_copy(b, c, send, target).start())
            return run

        on(low >= 0, dense_from(low, up_sem, above, has_above))
        on(high < zs, dense_from(high, down_sem, below, has_below))

        def hot_from(b, c, column, send, target, onward, sidewards):
            def run():
                block = b * PAIR + column
                hot_copy(block, c, send, target).wait_recv()
                on(onward, lambda: hot_copy(block, c, send, target).start())
                if sidewards:
                    hot_copy(block, c, hot_x, side).start()
            return run

        for c in order:
            columns = (x,) if c < hot_first else (x, 1 - x)
            for column in columns:
                on(low >= 0, hot_from(low, c, column, hot_up, above, has_above, c < hot_first))
                on(high < zs, hot_from(high, c, column, hot_down, below, has_below, c < hot_first))

    loop(1, zs, both_ways)

    reduced = z_buf[0].astype(jnp.float32)
    for b in range(1, zs):
        reduced = reduced + z_buf[b].astype(jnp.float32)
    G_ref[slot(core, q), :] = reduced.astype(WIRE).reshape(piece, -1)

    def gather_copy(k, quad_at):
        return pltpu.make_async_remote_copy(
            src_ref=G_ref.at[slot(core, quad_at)], dst_ref=G_ref.at[slot(core, quad_at)],
            send_sem=gather_send.at[k], recv_sem=gather_recv.at[quad_at],
            device_id=plane_peer(k)[1], device_id_type=MESH,
        )

    def twin_copy(core_at, quad_at):
        return pltpu.make_async_remote_copy(
            src_ref=G_ref.at[slot(core_at, quad_at)], dst_ref=G_ref.at[slot(core_at, quad_at)],
            send_sem=twin_send.at[quad_at], recv_sem=twin_recv.at[quad_at],
            device_id=twin, device_id_type=MESH,
        )

    for k in range(1, quads):
        gather_copy(k, q).start()
    twin_copy(core, q).start()

    for copy in dloads[1:4]:
        copy.wait()

    def dense_piece(core_at, quad_at):
        here = slot(core_at, quad_at)
        m, v, heading = moments(G_ref[here, :].astype(jnp.float32), dm_buf[here, :], dv_buf[here, :])
        dm_out[here, :] = m
        dv_out[here, :] = v
        U_buf[here, :] = heading
        usqs[core_at * quads + quad_at] = fold(heading * heading)

    weight_sq = full_sum(fold(dw_buf[...] * dw_buf[...]))
    dense_piece(core, q)
    for k in range(1, quads):
        other = plane_peer(k)[0]
        gather_copy(k, other).wait_recv()
        twin_copy(core, other).start()
        dense_piece(core, other)
    for k in range(quads):
        other = lax.rem(q + k, quads)
        twin_copy(1 - core, other).wait_recv()
        dense_piece(1 - core, other)
    dense_scale = trust_step(weight_sq, full_sum(jnp.sum(usqs[...], axis=0)))
    dw_out[...] = dw_buf[...] - dense_scale * U_buf[...]

    def hot_wait_side(b):
        for c in range(hot_first):
            hot_copy(b * PAIR + 1 - x, c, hot_x, side).wait_recv()
            hot_copy(b * PAIR + x, c, hot_x, side).wait_send()

    loop(0, zs, hot_wait_side)
    for c in range(hot_first, hot_chunks):
        hot_copy(d, c, hot_x, side).wait_send()
    for k in range(quads):
        core_copy(k).wait_send()
        twin_copy(core, k).wait_send()
    for k in range(1, quads):
        gather_copy(k, q).wait_send()
        plane_copy(k, 0, q).wait_send()
    for k in range(1, n_rows):
        sum_copy(k, r).wait_send()

    def sent(b):
        def run(z_sem, hot_sem, target):
            def go():
                for c in range(z_chunks):
                    z_copy(b, c, z_sem, target).wait_send()
                for c in range(hot_chunks):
                    hot_copy(b * PAIR + x, c, hot_sem, target).wait_send()
                    if c >= hot_first:
                        hot_copy(b * PAIR + 1 - x, c, hot_sem, target).wait_send()
            return go

        on(jnp.logical_and(has_above, b <= z), run(up_sem, hot_up, above))
        on(jnp.logical_and(has_below, b >= z), run(down_sem, hot_down, below))

    loop(0, zs, sent)


def write_out(n, *refs):
    sources, targets, sem = refs[:n], refs[n:2 * n], refs[2 * n]
    copies = [
        pltpu.make_async_copy(src, dst, sem.at[i])
        for i, (src, dst) in enumerate(zip(sources, targets))
    ]
    for copy in copies:
        copy.start()
    for copy in copies:
        copy.wait()


def shards(
    n_rows,
    n_dp,
    emb_weight,
    emb_grad,
    emb_moment,
    emb_second,
    hot_rows,
    block_counts,
    dense_weight,
    dense_grad,
    dense_moment,
    dense_second,
):
    _, rs, e = emb_weight.shape
    din, dout = dense_weight.shape
    hot_n = hot_rows.shape[2]
    quads, zs = n_rows // CORES * PAIR, n_dp // PAIR
    half = din // CORES
    piece = half // quads
    chunks = 6 if rs % (6 * 16) == 0 else 1
    hot_first, hot_chunks = 2, 4
    z_chunks = 2
    f32 = jnp.float32
    dma = pltpu.SemaphoreType.DMA
    vmem = pl.BlockSpec(memory_space=pltpu.VMEM)
    hbm = pl.BlockSpec(memory_space=pltpu.HBM)
    shapes = (
        jax.ShapeDtypeStruct((1, rs, e), f32),
        jax.ShapeDtypeStruct((1, rs, e), f32),
        jax.ShapeDtypeStruct((1, rs, e), f32),
        jax.ShapeDtypeStruct((n_dp, 1, hot_n, e), jnp.bfloat16),
        jax.ShapeDtypeStruct((din, dout), f32),
        jax.ShapeDtypeStruct((din, dout), f32),
        jax.ShapeDtypeStruct((din, dout), f32),
    )
    outs = pl.pallas_call(
        functools.partial(exchange, n_rows, n_dp, chunks, hot_first, hot_chunks, z_chunks),
        out_shape=tuple(pltpu.VMEM(shape.shape, shape.dtype) for shape in shapes),
        in_specs=[pl.BlockSpec(memory_space=pltpu.SMEM)] + [hbm] * 9,
        out_specs=(vmem,) * 7,
        scratch_shapes=[
            pltpu.SMEM(hot_rows.shape, jnp.int32),
            pltpu.VMEM((rs, e), f32),
            pltpu.VMEM((rs, e), emb_grad.dtype),
            pltpu.VMEM((rs, e), f32),
            pltpu.VMEM((rs, e), f32),
            pltpu.VMEM((rs, e), f32),
            pltpu.VMEM((din, dout), f32),
            pltpu.VMEM((din, dout), f32),
            pltpu.VMEM((din, dout), f32),
            pltpu.VMEM((din, dout), f32),
            pltpu.VMEM((din, dout), WIRE),
            pltpu.VMEM((din, dout), f32),
            pltpu.VMEM((quads, piece, dout), WIRE),
            pltpu.VMEM((quads, piece, dout), WIRE),
            pltpu.VMEM((quads, piece, dout), WIRE),
            pltpu.VMEM((quads, piece, dout), WIRE),
            pltpu.VMEM((zs, z_chunks, piece // z_chunks, dout), WIRE),
            pltpu.VMEM((n_rows, 2, 8, e), f32),
            pltpu.VMEM((CORES * quads, 8, dout), f32),
            pltpu.VMEM((hot_n, e), f32),
            pltpu.VMEM((hot_n, e), f32),
            dma((4, chunks)),
            dma((5,)),
            dma((quads,)),
            dma((quads,)),
            dma((quads,)),
            dma((quads,)),
            dma((zs, z_chunks)),
            dma((zs, z_chunks)),
            dma((zs, z_chunks)),
            dma((quads,)),
            dma((quads,)),
            dma((quads,)),
            dma((quads,)),
            dma((n_rows,)),
            dma((n_rows,)),
            dma((n_dp, hot_chunks)),
            dma((n_dp, hot_chunks)),
            dma((n_dp, hot_chunks)),
            dma((n_dp, hot_chunks)),
        ],
        compiler_params=pltpu.CompilerParams(
            collective_id=0, has_side_effects=True, vmem_limit_bytes=EXCHANGE_LIMIT
        ),
        name="exchange",
    )(
        block_counts,
        *(
            pltpu.with_memory_space_constraint(a, pltpu.HBM)
            for a in (
                hot_rows, emb_weight, emb_grad, emb_moment, emb_second,
                dense_grad, dense_weight, dense_moment, dense_second,
            )
        ),
    )
    return pl.pallas_call(
        functools.partial(write_out, len(shapes)),
        out_shape=shapes,
        in_specs=[vmem] * len(shapes),
        out_specs=(hbm,) * len(shapes),
        scratch_shapes=[dma((len(shapes),))],
        compiler_params=pltpu.CompilerParams(vmem_limit_bytes=WRITE_LIMIT),
        name="write_out",
    )(*outs)


def solution(mesh):
    in_specs = (
        P("dp", "rows", None),
        P("dp", "rows", None),
        P("dp", "rows", None),
        P("dp", "rows", None),
        P("dp", "rows", None),
        P("dp", "rows"),
        P(),
        P(("rows", "dp"), None, None),
        P(),
        P(),
    )
    out_specs = (
        P("dp", "rows", None),
        P("dp", "rows", None),
        P("dp", "rows", None),
        P(None, "rows", None, None),
        P(),
        P(),
        P(),
    )
    body = functools.partial(shards, mesh.shape["rows"], mesh.shape["dp"])
    return jax.shard_map(body, mesh=mesh, in_specs=in_specs, out_specs=out_specs, check_vma=False)
```

time: 45.6 us -> 33 us (0.72)
  local copies, waits for them, and re-layouts: 6.77 us -> 0 us
  other arithmetic: 5.3 us -> 0 us
  between operations: 2.73 us -> 1.29 us
  Pallas kernels: 30.4 us -> 31.4 us
    unnamed x23 -> x0, local copies, waits for them, and re-layouts: 6.25 us -> none
    sub x2 -> x0, other arithmetic: 3.58 us -> none  [the longest x1 2.54 us: shards(): new_weight = emb_weight - step_size[0, 0] * update]
    reduce_sum x2 -> x0, other arithmetic: 1.72 us -> none  [the longest x1 0.98 us: shards(): jnp.sum(heading * heading)]
    pallas_call x1 -> x2, Pallas kernels: 30.4 us -> 31.4 us  [the longest x1 29.2 us: shards(): pl.pallas_call(functools.partial(exchange, n_rows, n_dp, chunks, hot_firs...]
    slice x1 -> x0, local copies, waits for them, and re-layouts: 0.51 us -> none  [shards(): new_weight = emb_weight - step_size[0, 0] * update]
where the time goes in v2:
time: 33 us; the launch traced here: 32.7 us
  Pallas kernels  31.4 us (95%)
  between operations  1.29 us (4%)
    pallas_call x1, Pallas kernels, shards(): pl.pallas_call(functools.partial(exchange, n_rows, n_dp, chunks, hot_firs...  29.2 us
    pallas_call x1, Pallas kernels, shards(): pl.pallas_call(functools.partial(write_out, len(shapes)), out_shape=shape...  2.15 us

profile of v2, /device:TPU:0, one launch (start us, length us, event | category | flops | bytes accessed | tf_op | source)
XLA Modules:
  0.0 32.7 jit_solution(4885235035012601341)
XLA Ops:
  1.3 29.2 %exchange.1 = (f32[1,1536,128]{2,1,0:T(8,128)S(1)}, f32[1,1536,128]{2,1,0:T(8,128)S(1)}, f32[1,1536,128]{2,1,0:T(8,128)S(1)}, bf16[8,1,256,128]{3,2,1,0:T(8,128)...) custom-call(s32[1,1]{1,0:T(1,128)S(6)} %copy.17.count_ref, ...), custom_call_target="tpu_custom_call" | custom-call | tf_op jit(solution)/shard_map/exchange/pallas_call | solution.py:440
  30.5 2.2 %write_out.1 = (f32[1,1536,128]{2,1,0:T(8,128)}, f32[1,1536,128]{2,1,0:T(8,128)}, f32[1,1536,128]{2,1,0:T(8,128)}, bf16[8,1,256,128]{3,2,1,0:T(8,128)(2,1)}, f32...) custom-call(f32[1,1536,128]{2,1,0:T(8,128)S(1)} %get-tuple-element.14.refs_0_, ...), custom_call_target="tpu_custom_call" | custom-call | tf_op jit(solution)/shard_map/write_out/pallas_call | solution.py:501

commit v3 on v2

--- a/solution.py
+++ b/solution.py
@@ -23,6 +23,7 @@
 CORES = 2
 PAIR = 2
 WIRE = jnp.bfloat16
+LATE = 1
 EXCHANGE_LIMIT = 40 * 1024 * 1024
 WRITE_LIMIT = 1024 * 1024
 
@@ -55,12 +56,12 @@
 
 
 def exchange(
-    n_rows, n_dp, chunks, hot_first, hot_chunks, z_chunks,
+    n_rows, n_dp, chunks, hot_first, hot_chunks,
     count_ref, rows_hbm, w_hbm, g_hbm, m_hbm, v_hbm, dg_hbm, dw_hbm, dm_hbm, dv_hbm,
     w_out, m_out, v_out, hot_ref, dw_out, dm_out, dv_out,
     rows_ref, w_buf, g_buf, m_buf, v_buf, u_buf, dg_buf, dw_buf, dm_buf, dv_buf, G_ref, U_buf,
     core_out, core_in, plane_out, plane_in, z_buf, sums, usqs, hot_w, hot_u,
-    load_sem, dload_sem, core_send, core_recv, plane_send, plane_recv, up_sem, down_sem, z_recv,
+    load_sem, dload_sem, core_send, core_recv, plane_send, plane_recv, z_send, z_recv,
     gather_send, gather_recv, twin_send, twin_recv,
     sum_send, sum_recv, hot_up, hot_down, hot_x, hot_recv,
 ):
@@ -80,6 +81,10 @@
         oy, ox = lax.div(other, PAIR), lax.rem(other, PAIR)
         return other, (oy * CORES + core, z * PAIR + ox)
 
+    def line_peer(k):
+        other = lax.rem(z + k, zs)
+        return other, (r, other * PAIR + x)
+
     def row_peer(k):
         other = lax.rem(r + k, n_rows)
         return other, (other, d)
@@ -122,17 +127,10 @@
         )
         greeted += 1
 
-    @pl.when(has_above)
-    def _():
-        pl.semaphore_signal(barrier, inc=1, device_id=above, device_id_type=MESH)
-
-    @pl.when(has_below)
-    def _():
-        pl.semaphore_signal(barrier, inc=1, device_id=below, device_id_type=MESH)
-
-    pl.semaphore_wait(
-        barrier, greeted + has_above.astype(jnp.int32) + has_below.astype(jnp.int32)
-    )
+    for k in range(1, zs):
+        pl.semaphore_signal(barrier, inc=1, device_id=line_peer(k)[1], device_id_type=MESH)
+        greeted += 1
+    pl.semaphore_wait(barrier, greeted)
 
     half = dg_buf.shape[0] // CORES
     piece = half // quads
@@ -199,20 +197,6 @@
     for k in range(1, n_rows):
         sum_copy(k, r).start()
 
-    core_copy(q).wait_recv()
-    own = dg_buf[slot(core, q), :] + core_in[q].astype(jnp.float32)
-    for k in range(1, quads):
-        other = plane_peer(k)[0]
-        plane_copy(k, 0, other).wait_recv()
-        own = own + plane_in[other].astype(jnp.float32)
-    z_buf[z] = own.astype(WIRE).reshape(z_buf.shape[1:])
-
-    def z_copy(b, c, send, target):
-        return pltpu.make_async_remote_copy(
-            src_ref=z_buf.at[b, c], dst_ref=z_buf.at[b, c],
-            send_sem=send.at[b, c], recv_sem=z_recv.at[b, c], device_id=target, device_id_type=MESH,
-        )
-
     hot_rows_at = hot_ref.shape[2] // hot_chunks
 
     def hot_copy(block, c, send, target):
@@ -227,16 +211,6 @@
         @pl.when(condition)
         def _():
             action()
-
-    def z_all(b, up, down):
-        for c in range(z_chunks):
-            if up:
-                z_copy(b, c, up_sem, above).start()
-            if down:
-                z_copy(b, c, down_sem, below).start()
-
-    on(has_above, lambda: z_all(z, True, False))
-    on(has_below, lambda: z_all(z, False, True))
 
     hot_n = hot_w.shape[0]
 
@@ -264,6 +238,24 @@
         on(has_above, lambda: hot_copy(d, c, hot_up, above).start())
         on(has_below, lambda: hot_copy(d, c, hot_down, below).start())
 
+    core_copy(q).wait_recv()
+    own = dg_buf[slot(core, q), :] + core_in[q].astype(jnp.float32)
+    for k in range(1, quads):
+        other = plane_peer(k)[0]
+        plane_copy(k, 0, other).wait_recv()
+        own = own + plane_in[other].astype(jnp.float32)
+    z_buf[z] = own.astype(WIRE)
+
+    def z_copy(k, slot_at):
+        return pltpu.make_async_remote_copy(
+            src_ref=z_buf.at[slot_at], dst_ref=z_buf.at[slot_at],
+            send_sem=z_send.at[k], recv_sem=z_recv.at[slot_at],
+            device_id=line_peer(k)[1], device_id_type=MESH,
+        )
+
+    for k in range(1, zs):
+        z_copy(k, z).start()
+
     def renew(c, carry):
         here = pl.ds(pl.multiple_of(c * span, span), span)
         w_out[0, here, :] = w_buf[here, :] - scale * u_buf[here, :]
@@ -279,16 +271,6 @@
 
     def both_ways(k):
         low, high = z - k, z + k
-
-        def dense_from(b, send, target, onward):
-            def run():
-                for c in range(z_chunks):
-                    z_copy(b, c, send, target).wait_recv()
-                    on(onward, lambda: z_copy(b, c, send, target).start())
-            return run
-
-        on(low >= 0, dense_from(low, up_sem, above, has_above))
-        on(high < zs, dense_from(high, down_sem, below, has_below))
 
         def hot_from(b, c, column, send, target, onward, sidewards):
             def run():
@@ -305,12 +287,15 @@
                 on(low >= 0, hot_from(low, c, column, hot_up, above, has_above, c < hot_first))
                 on(high < zs, hot_from(high, c, column, hot_down, below, has_below, c < hot_first))
 
-    loop(1, zs, both_ways)
-
+    last = max(1, zs - LATE)
+    loop(1, last, both_ways)
+
+    for k in range(1, zs):
+        z_copy(k, line_peer(k)[0]).wait_recv()
     reduced = z_buf[0].astype(jnp.float32)
     for b in range(1, zs):
         reduced = reduced + z_buf[b].astype(jnp.float32)
-    G_ref[slot(core, q), :] = reduced.astype(WIRE).reshape(piece, -1)
+    G_ref[slot(core, q), :] = reduced.astype(WIRE)
 
     def gather_copy(k, quad_at):
         return pltpu.make_async_remote_copy(
@@ -329,6 +314,8 @@
     for k in range(1, quads):
         gather_copy(k, q).start()
     twin_copy(core, q).start()
+
+    loop(last, zs, both_ways)
 
     for copy in dloads[1:4]:
         copy.wait()
@@ -371,20 +358,20 @@
         plane_copy(k, 0, q).wait_send()
     for k in range(1, n_rows):
         sum_copy(k, r).wait_send()
+    for k in range(1, zs):
+        z_copy(k, z).wait_send()
 
     def sent(b):
-        def run(z_sem, hot_sem, target):
+        def run(hot_sem, target):
             def go():
-                for c in range(z_chunks):
-                    z_copy(b, c, z_sem, target).wait_send()
                 for c in range(hot_chunks):
                     hot_copy(b * PAIR + x, c, hot_sem, target).wait_send()
                     if c >= hot_first:
                         hot_copy(b * PAIR + 1 - x, c, hot_sem, target).wait_send()
             return go
 
-        on(jnp.logical_and(has_above, b <= z), run(up_sem, hot_up, above))
-        on(jnp.logical_and(has_below, b >= z), run(down_sem, hot_down, below))
+        on(jnp.logical_and(has_above, b <= z), run(hot_up, above))
+        on(jnp.logical_and(has_below, b >= z), run(hot_down, below))
 
     loop(0, zs, sent)
 
@@ -422,8 +409,7 @@
     half = din // CORES
     piece = half // quads
     chunks = 6 if rs % (6 * 16) == 0 else 1
-    hot_first, hot_chunks = 2, 4
-    z_chunks = 2
+    hot_first, hot_chunks = 4, 4
     f32 = jnp.float32
     dma = pltpu.SemaphoreType.DMA
     vmem = pl.BlockSpec(memory_space=pltpu.VMEM)
@@ -438,7 +424,7 @@
         jax.ShapeDtypeStruct((din, dout), f32),
     )
     outs = pl.pallas_call(
-        functools.partial(exchange, n_rows, n_dp, chunks, hot_first, hot_chunks, z_chunks),
+        functools.partial(exchange, n_rows, n_dp, chunks, hot_first, hot_chunks),
         out_shape=tuple(pltpu.VMEM(shape.shape, shape.dtype) for shape in shapes),
         in_specs=[pl.BlockSpec(memory_space=pltpu.SMEM)] + [hbm] * 9,
         out_specs=(vmem,) * 7,
@@ -459,7 +445,7 @@
             pltpu.VMEM((quads, piece, dout), WIRE),
             pltpu.VMEM((quads, piece, dout), WIRE),
             pltpu.VMEM((quads, piece, dout), WIRE),
-            pltpu.VMEM((zs, z_chunks, piece // z_chunks, dout), WIRE),
+            pltpu.VMEM((zs, piece, dout), WIRE),
             pltpu.VMEM((n_rows, 2, 8, e), f32),
             pltpu.VMEM((CORES * quads, 8, dout), f32),
             pltpu.VMEM((hot_n, e), f32),
@@ -470,9 +456,8 @@
             dma((quads,)),
             dma((quads,)),
             dma((quads,)),
-            dma((zs, z_chunks)),
-            dma((zs, z_chunks)),
-            dma((zs, z_chunks)),
+            dma((zs,)),
+            dma((zs,)),
             dma((quads,)),
             dma((quads,)),
             dma((quads,)),

time: 33 us -> 28.8 us (0.87)
  Pallas kernels: 31.4 us -> 27.4 us
    pallas_call x1, Pallas kernels: 29.2 us -> 25.2 us  [shards(): pl.pallas_call(functools.partial(exchange, n_rows, n_dp, chunks, hot_firs...]
where the time goes in v3:
time: 28.8 us; the launch traced here: 28.6 us
  Pallas kernels  27.4 us (95%)
  between operations  1.29 us (4%)
    pallas_call x1, Pallas kernels, shards(): pl.pallas_call(functools.partial(exchange, n_rows, n_dp, chunks, hot_firs...  25.2 us
    pallas_call x1, Pallas kernels, shards(): pl.pallas_call(functools.partial(write_out, len(shapes)), out_shape=shape...  2.15 us

profile of v3, /device:TPU:0, one launch (start us, length us, event | category | flops | bytes accessed | tf_op | source)
XLA Modules:
  0.0 28.6 jit_solution(7306285918637662831)
XLA Ops:
  1.3 25.2 %exchange.1 = (f32[1,1536,128]{2,1,0:T(8,128)S(1)}, f32[1,1536,128]{2,1,0:T(8,128)S(1)}, f32[1,1536,128]{2,1,0:T(8,128)S(1)}, bf16[8,1,256,128]{3,2,1,0:T(8,128)...) custom-call(s32[1,1]{1,0:T(1,128)S(6)} %copy.17.count_ref, ...), custom_call_target="tpu_custom_call" | custom-call | tf_op jit(solution)/shard_map/exchange/pallas_call | solution.py:426
  26.5 2.2 %write_out.1 = (f32[1,1536,128]{2,1,0:T(8,128)}, f32[1,1536,128]{2,1,0:T(8,128)}, f32[1,1536,128]{2,1,0:T(8,128)}, bf16[8,1,256,128]{3,2,1,0:T(8,128)(2,1)}, f32...) custom-call(f32[1,1536,128]{2,1,0:T(8,128)S(1)} %get-tuple-element.14.refs_0_, ...), custom_call_target="tpu_custom_call" | custom-call | tf_op jit(solution)/shard_map/write_out/pallas_call | solution.py:486
